TPU v7x, 32 devices: a whole 2x2x4 slice. The times are simulated.
32 devices in a mesh: parts: 2 (over x), chol: 16 (over z, y, core).
Axes of the slice: x: 2, y: 2, z: 4, core: 2. Of those that a mesh axis runs over, the one named last changes fastest.
Arguments:
- orbitals: float32 [32, 100, 1024], P(('parts', 'chol')), parts along dimension 0, may hold values from -6 to 6
- intersection_inv: float32 [32, 100, 100], P(('parts', 'chol')), parts along dimension 0, may hold values from -0.625 to 0.625
- factor_rows: bfloat16 [4096, 1024], P('chol'), may hold values from -0.1875 to 0.1875
- factor_rotated: bfloat16 [100, 4096], replicated, may hold values from -0.625 to 0.625
- factor_core: bfloat16 [1024, 4096], P('chol'), may hold values from -0.125 to 0.125
- fields: float32 [32, 1024], P('parts', 'chol'), parts along dimension 0, may hold values from -6 to 6
Outputs:
- propagated: float32 [32, 100, 1024], P(('parts', 'chol')), parts along dimension 0
- force_bias: float32 [32, 1024], P('parts', 'chol'), parts along dimension 0
There are 2 independent parts, one for each index of `parts`. A program takes and returns all parts, laid end to end along the dimension named above; an argument that names none is the same for every part. Nothing has to cross between parts.
All inputs are finite; a program needn't handle non-finite values.
Results may differ from a plain program's by a relative error of at most 0.0091.
Values may be sent and summed in bfloat16 or wider, within the bound.
A program may use at most 64 MiB of HBM per device.

v0:
```python
import jax
import jax.numpy as jnp
from jax import lax
from jax.sharding import PartitionSpec as P

TAYLOR = 4


def density_one(half_green, all_rows, factor_rotated):
    projected = lax.dot_general(
        half_green, all_rows, (((1,), (1,)), ((), ())), preferred_element_type=jnp.float32
    )
    return jnp.sum(factor_rotated.astype(jnp.float32) * projected, axis=0).astype(jnp.bfloat16)


def propagate_one(orbital, potential, all_rows):
    total = orbital
    term = orbital
    for order in range(1, TAYLOR + 1):
        summed = lax.dot_general(
            term.astype(jnp.bfloat16),
            all_rows,
            (((1,), (1,)), ((), ())),
            preferred_element_type=jnp.float32,
        )
        scaled = (summed * potential[None, :] / order).astype(jnp.bfloat16)
        term = jnp.dot(scaled, all_rows, preferred_element_type=jnp.float32)
        total = total + term
    return total


def on_device(orbitals, intersection_inv, factor_rows, factor_rotated, factor_core, fields):
    walker_count = orbitals.shape[0]
    half_green = jnp.einsum(
        "wij,wjm->wim", intersection_inv, orbitals, precision=lax.Precision.HIGHEST
    ).astype(jnp.bfloat16)
    all_rows = lax.all_gather(factor_rows, "chol", axis=0, tiled=True)
    own_density = lax.map(lambda item: density_one(item, all_rows, factor_rotated), half_green)
    density = lax.all_gather(own_density, "chol", axis=0, tiled=True)
    force_bias = lax.dot_general(
        density, factor_core, (((1,), (1,)), ((), ())), preferred_element_type=jnp.float32
    )
    shifted = (fields - force_bias).astype(jnp.bfloat16)
    partial_sum = jnp.dot(shifted, factor_core, preferred_element_type=jnp.float32)
    summed_all = lax.psum(partial_sum, "chol")
    potential = lax.dynamic_slice_in_dim(
        summed_all, lax.axis_index("chol") * walker_count, walker_count, 0
    )
    propagated = lax.map(
        lambda pair: propagate_one(pair[0], pair[1], all_rows), (orbitals, potential)
    )
    return (propagated, force_bias)


def solution(mesh):
    in_specs = (
        P(("parts", "chol"), None, None),
        P(("parts", "chol"), None, None),
        P("chol", None),
        P(),
        P("chol", None),
        P("parts", "chol"),
    )
    out_specs = (P(("parts", "chol"), None, None), P("parts", "chol"))
    return jax.shard_map(
        on_device, mesh=mesh, in_specs=in_specs, out_specs=out_specs, check_vma=False
    )
```

profile of v0, /device:TPU:0, one launch (start us, length us, event | category | flops | bytes accessed | tf_op | source)
XLA Modules:
  0.0 249.2 jit_solution(8666170632495442712)
XLA Ops:
  7.2 0.0 copy-start
  7.2 0.0 copy-start.1
  7.2 0.0 copy-start.3
  7.2 0.0 all-gather.3.cloned.1.call-start
  7.2 0.7 all-gather.3.cloned.1.call-update
  7.9 0.0 all-reduce.2.cloned.1.call-start
  8.0 1.6 convolution_convert_fusion
  9.6 77.7 %all-gather.3.cloned.1.call-done = bf16[4096,1024]{1,0:T(8,128)(2,1)} async-done(((bf16[256,1024]{1,0:T(8,128)(2,1)}), bf16[4096,1024]{1,0:T(8,128)(2,1)}) %all-gather.3.cloned.1.call-update) | async-done | bytes 8388624 | tf_op jit(solution)/shard_map/all_gather | solution.py:37
  87.2 6.3 %fusion.7 = bf16[4096]{0:T(1024)(128)(2,1)S(1)} fusion(bf16[100,1024]{1,0:T(8,128)(2,1)S(1)} %convolution_convert_fusion, bf16[4096,1024]{1,0:T(8,128)(2,1)} %all-gather.3.cloned.1.call-done, bf16[100,4096]{1,0:T(8,128)(2,1)} %param.9), kind=kOutput, calls=%fused_computation.12 | convolution fusion | flops 840085504 | bytes 9420800 | tf_op jit(solution)/shard_map/while/body/eval_jaxpr/dot_general | solution.py:10
  93.5 19.5 %all-gather = bf16[65536]{0:T(1024)(128)(2,1)S(1)} all-gather(bf16[4096]{0:T(1024)(128)(2,1)S(1)} %fusion.7), channel_id=2, replica_groups=mesh['parts'=2,'chol'=16] {'chol'}, dimensions={0}, use_global_device_ids=true | all-gather | bytes 139264 | tf_op jit(solution)/shard_map/all_gather | solution.py:39
  113.0 0.1 reshape.20
  113.1 0.0 copy-done
  113.1 0.2 fusion.28
  113.3 0.0 copy-done.3
  113.3 0.0 copy-start.2
  113.3 0.9 fusion.24
  114.2 0.0 all-reduce.2.cloned.1.call-update
  114.3 87.1 %all-reduce.2.cloned.1.call-done = f32[16,4096]{1,0:T(8,128)} async-done(((f32[16,4096]{1,0:T(8,128)}), f32[16,4096]{1,0:T(8,128)}) %all-reduce.2.cloned.1.call-update) | async-done | bytes 262160 | tf_op jit(solution)/shard_map/psum | solution.py:45
  201.4 0.9 constant_dynamic-slice_fusion
  202.3 0.0 copy-done.1
  202.3 9.7 %fusion.11 = f32[100,1024]{1,0:T(8,128)S(1)} fusion(bf16[4096,1024]{1,0:T(8,128)(2,1)} %all-gather.3.cloned.1.call-done, f32[4096]{0:T(1024)S(1)} %bitcast.32, f32[1,100,1024]{2,0,1:T(1,128)S(1)} %copy-done.1), kind=kOutput, calls=%fused_computation.18 | convolution fusion | flops 1678540800 | bytes 9224192 | tf_op jit(solution)/shard_map/while/body/eval_jaxpr/dot_general | solution.py:27
  212.0 0.0 copy-done.2
  212.0 9.7 %fusion.10 = f32[100,1024]{1,0:T(8,128)S(1)} fusion(bf16[4096,1024]{1,0:T(8,128)(2,1)} %all-gather.3.cloned.1.call-done, f32[4096]{0:T(1024)S(1)} %bitcast.33, f32[100,1024]{1,0:T(8,128)S(1)} %fusion.11), kind=kOutput, calls=%fused_computation.17 | convolution fusion | flops 1679052800 | bytes 9224192 | tf_op jit(solution)/shard_map/while/body/eval_jaxpr/dot_general | solution.py:27
  221.7 9.7 %fusion.9 = f32[100,1024]{1,0:T(8,128)S(1)} fusion(bf16[4096,1024]{1,0:T(8,128)(2,1)} %all-gather.3.cloned.1.call-done, f32[4096]{0:T(1024)S(1)} %bitcast.34, f32[100,1024]{1,0:T(8,128)S(1)} %fusion.10), kind=kOutput, calls=%fused_computation.16 | convolution fusion | flops 1679052800 | bytes 9224192 | tf_op jit(solution)/shard_map/while/body/eval_jaxpr/dot_general | solution.py:27
  231.5 9.7 %fusion.8 = f32[1,100,1024]{2,1,0:T(8,128)S(1)} fusion(bf16[4096,1024]{1,0:T(8,128)(2,1)} %all-gather.3.cloned.1.call-done, f32[4096]{0:T(1024)S(1)} %bitcast.35, f32[100,1024]{1,0:T(8,128)S(1)} %fusion.9, f32[100,1024]{1,0:T(8,128)S(1)} %fusion.10, f32[100,1024]{1,0:T(8,128)S(1)} %fusion.11, f32[1,100,1024]{2,0,1:T(1,128)S(1)} %copy-done.1), kind=kOutput, calls=%fused_computation.14 | convolution fusion | flops 1679462400 | bytes 10452992 | tf_op jit(solution)/shard_map/while/body/eval_jaxpr/dot_general | solution.py:27
  241.2 1.2 copy.9
Async XLA Ops:
  7.2 105.9 %copy-start = (bf16[64,4096]{1,0:T(8,128)(2,1)S(1)}, bf16[64,4096]{1,0:T(8,128)(2,1)}, u32[]{:S(2)}) copy-start(bf16[64,4096]{1,0:T(8,128)(2,1)} %param.10) | copy-start | bytes 1572868
  7.2 195.2 %copy-start.1 = (f32[1,100,1024]{2,0,1:T(1,128)S(1)}, f32[1,100,1024]{2,0,1:T(1,128)}, u32[]{:S(2)}) copy-start(f32[1,100,1024]{2,0,1:T(1,128)} %param.6) | copy-start | bytes 1228804
  7.2 106.1 %copy-start.3 = (f32[16,64]{1,0:T(8,128)S(1)}, f32[16,64]{1,0:T(8,128)}, u32[]{:S(2)}) copy-start(f32[16,64]{1,0:T(8,128)} %param.11) | copy-start | bytes 12292
  7.2 80.0 %all-gather.3.cloned.1.call-start = ((), (), s32[]{:S(2)}) async-start(), calls=%async_computation | async-start | bytes 8912896 | tf_op jit(solution)/shard_map/all_gather | solution.py:37
  7.9 193.5 %all-reduce.2.cloned.1.call-start = ((), (), s32[]{:S(2)}) async-start(), calls=%async_computation.1 | async-start | bytes 524288 | tf_op jit(solution)/shard_map/psum | solution.py:45
  113.3 98.7 %copy-start.2 = (f32[16,64]{1,0:T(8,128)}, f32[16,64]{1,0:T(8,128)S(1)}, u32[]{:S(2)}) copy-start(f32[16,64]{1,0:T(8,128)S(1)} %fusion.28) | copy-start | bytes 12292
Sparse Core Ops, SparseCore 0:
  10.2 77.0 all-gather.2
  114.4 86.9 all-reduce.1
where the time goes:
time: 249 us
  waiting for transfers between devices  166 us (67%)
  matrix products  47.9 us (19%)
  blocking collectives  19.5 us (8%)
  between operations  14.1 us (6%)
    psum x1, waiting for transfers between devices, on_device(): summed_all = lax.psum(partial_sum, 'chol')  87.1 us
    all_gather x1, waiting for transfers between devices, on_device(): all_rows = lax.all_gather(factor_rows, 'chol', axis=0, tiled=True)  77.7 us
    dot_general x4, matrix products, propagate_one(): term = jnp.dot(scaled, all_rows, preferred_element_type=jnp.float32)  38.9 us
    all_gather x1, blocking collectives, on_device(): density = lax.all_gather(own_density, 'chol', axis=0, tiled=True)  19.5 us
    dot_general x1, matrix products, density_one(): lax.dot_general(half_green, all_rows, (((1,), (1,)), ((), ())), preferred...  6.26 us
  transfers between devices with their start and end apart: 2, of which 2 were waited for; matrix products, arithmetic and copies ran while one was open for 1% of the time, Pallas kernels for 0%

commit v1 on v0

--- a/solution.py
+++ b/solution.py
@@ -4,6 +4,19 @@
 from jax.sharding import PartitionSpec as P
 
 TAYLOR = 4
+
+
+def ring_gather(x, axis, dim):
+    ways = lax.axis_size(axis)
+    up = [(d, (d + 1) % ways) for d in range(ways)]
+    down = [(d, (d - 1) % ways) for d in range(ways)]
+    earlier, later = ([x], [x])
+    for _ in range(ways // 2):
+        earlier.append(lax.ppermute(earlier[-1], axis, up))
+    for _ in range((ways - 1) // 2):
+        later.append(lax.ppermute(later[-1], axis, down))
+    line = jnp.concatenate([*earlier[::-1], *later[1:]], axis=dim)
+    return jnp.roll(line, (lax.axis_index(axis) - ways // 2) * x.shape[dim], axis=dim)
 
 
 def density_one(half_green, all_rows, factor_rotated):
@@ -34,7 +47,7 @@
     half_green = jnp.einsum(
         "wij,wjm->wim", intersection_inv, orbitals, precision=lax.Precision.HIGHEST
     ).astype(jnp.bfloat16)
-    all_rows = lax.all_gather(factor_rows, "chol", axis=0, tiled=True)
+    all_rows = ring_gather(factor_rows, "chol", 0)
     own_density = lax.map(lambda item: density_one(item, all_rows, factor_rotated), half_green)
     density = lax.all_gather(own_density, "chol", axis=0, tiled=True)
     force_bias = lax.dot_general(

time: 249 us -> 302 us (1.21)
  starting transfers between devices: 0.08 us -> 44.7 us
  waiting for transfers between devices: 166 us -> 137 us
  local copies, waits for them, and re-layouts: 2.17 us -> 25.6 us
  blocking collectives: 19.5 us -> 31.5 us
    all_gather x1 -> x0, waiting for transfers between devices: 77.7 us -> none  [on_device(): all_rows = lax.all_gather(factor_rows, 'chol', axis=0, tiled=True)]
    ppermute x0 -> x15, waiting for transfers between devices: none -> 50.1 us  [the longest x8 50 us: ring_gather(): earlier.append(lax.ppermute(earlier[-1], axis, up))]
    ppermute x0 -> x15, starting transfers between devices: none -> 44.6 us  [the longest x8 31.9 us: ring_gather(): earlier.append(lax.ppermute(earlier[-1], axis, up))]
    unnamed x9 -> x68, local copies, waits for them, and re-layouts: 1.2 us -> 24.6 us
    all_gather x1, blocking collectives: 19.5 us -> 31.5 us  [on_device(): density = lax.all_gather(own_density, 'chol', axis=0, tiled=True)]
    dot_general x1, matrix products: 6.26 us -> 2.74 us  [density_one(): lax.dot_general(half_green, all_rows, (((1,), (1,)), ((), ())), preferred...]
  transfers between devices with their start and end apart: 2 -> 16, of which waited for: 2 -> 9; matrix products, arithmetic and copies ran while one was open for 1% -> 5% of each run, Pallas kernels for 0% -> 0%
where the time goes in v1:
time: 302 us; the launch traced here: 300 us
  waiting for transfers between devices  137 us (45%)
  matrix products  46.9 us (16%)
  starting transfers between devices  44.7 us (15%)
  blocking collectives  31.5 us (10%)
  local copies, waits for them, and re-layouts  25.6 us (8%)
  between operations  14.4 us (5%)
    psum x1, waiting for transfers between devices, on_device(): summed_all = lax.psum(partial_sum, 'chol')  87.2 us
    ppermute x8, waiting for transfers between devices, ring_gather(): earlier.append(lax.ppermute(earlier[-1], axis, up))  50 us
    dot_general x4, matrix products, propagate_one(): term = jnp.dot(scaled, all_rows, preferred_element_type=jnp.float32)  40.6 us
    ppermute x8, starting transfers between devices, ring_gather(): earlier.append(lax.ppermute(earlier[-1], axis, up))  31.9 us
    all_gather x1, blocking collectives, on_device(): density = lax.all_gather(own_density, 'chol', axis=0, tiled=True)  31.5 us
    unnamed x68, local copies, waits for them, and re-layouts  24.6 us
    ppermute x7, starting transfers between devices, ring_gather(): later.append(lax.ppermute(later[-1], axis, down))  12.7 us
  transfers between devices with their start and end apart: 16, of which 9 were waited for; matrix products, arithmetic and copies ran while one was open for 5% of the time, Pallas kernels for 0%

profile of v1, /device:TPU:0, one launch (start us, length us, event | category | flops | bytes accessed | tf_op | source)
XLA Modules:
  0.0 300.4 jit_solution(13919923498295640483)
XLA Ops:
  7.2 0.5 collective-permute-start
  7.8 12.1 %collective-permute-done = bf16[256,1024]{1,0:T(8,128)(2,1)S(1)} collective-permute-done((bf16[256,1024]{1,0:T(8,128)(2,1)}, bf16[256,1024]{1,0:T(8,128)(2,1)S(1)}, u32[]{:S(2)}, u32[]{:S(2)}) %collective-permute-start) | collective-permute-done | bytes 524320 | tf_op jit(solution)/shard_map/ppermute | solution.py:15
  19.8 4.4 %collective-permute-start.8 = (bf16[256,1024]{1,0:T(8,128)(2,1)}, bf16[256,1024]{1,0:T(8,128)(2,1)S(1)}, u32[]{:S(2)}, u32[]{:S(2)}) collective-permute-start(bf16[256,1024]{1,0:T(8,128)(2,1)} %param.8), channel_id=1, source_target_pairs={{0,15},{1,0},{2,1},{3,2},{4,3},{5,4},{6,5},{7,6},{8,7},{9,8},{10,9... | collective-permute-start | bytes 1572872 | tf_op jit(solution)/shard_map/ppermute | solution.py:17
  24.3 7.0 %collective-permute-done.1 = bf16[256,1024]{1,0:T(8,128)(2,1)S(1)} collective-permute-done((bf16[256,1024]{1,0:T(8,128)(2,1)S(1)}, bf16[256,1024]{1,0:T(8,128)(2,1)S(1)}, u32[]{:S(2)}, u32[]{:S(2)}) %collective-permute-start.1) | collective-permute-done | bytes 524320 | tf_op jit(solution)/shard_map/ppermute | solution.py:15
  31.3 4.6 %collective-permute-start.9 = (bf16[256,1024]{1,0:T(8,128)(2,1)S(1)}, bf16[256,1024]{1,0:T(8,128)(2,1)S(1)}, u32[]{:S(2)}, u32[]{:S(2)}) collective-permute-start(bf16[256,1024]{1,0:T(8,128)(2,1)S(1)} %collective-permute-done.8), channel_id=1, source_target_pairs={{0,15},{1,0},{2,1},{3,2},{4,3},{5,4},{6,5},{7,6},{8,7},{9,8},{10,9... | collective-permute-start | bytes 1572872 | tf_op jit(solution)/shard_map/ppermute | solution.py:17
  35.9 6.8 %collective-permute-done.2 = bf16[256,1024]{1,0:T(8,128)(2,1)S(1)} collective-permute-done((bf16[256,1024]{1,0:T(8,128)(2,1)S(1)}, bf16[256,1024]{1,0:T(8,128)(2,1)S(1)}, u32[]{:S(2)}, u32[]{:S(2)}) %collective-permute-start.2) | collective-permute-done | bytes 524320 | tf_op jit(solution)/shard_map/ppermute | solution.py:15
  42.7 1.8 collective-permute-start.3
  44.4 2.9 collective-permute-start.10
  47.3 6.8 %collective-permute-done.3 = bf16[256,1024]{1,0:T(8,128)(2,1)S(1)} collective-permute-done((bf16[256,1024]{1,0:T(8,128)(2,1)S(1)}, bf16[256,1024]{1,0:T(8,128)(2,1)S(1)}, u32[]{:S(2)}, u32[]{:S(2)}) %collective-permute-start.3) | collective-permute-done | bytes 524320 | tf_op jit(solution)/shard_map/ppermute | solution.py:15
  54.1 3.8 %collective-permute-start.4 = (bf16[256,1024]{1,0:T(8,128)(2,1)S(1)}, bf16[256,1024]{1,0:T(8,128)(2,1)S(1)}, u32[]{:S(2)}, u32[]{:S(2)}) collective-permute-start(bf16[256,1024]{1,0:T(8,128)(2,1)S(1)} %collective-permute-done.3), channel_id=1, source_target_pairs={{0,1},{1,2},{2,3},{3,4},{4,5},{5,6},{6,7},{7,8},{8,9},{9,10},{10,1... | collective-permute-start | bytes 1572872 | tf_op jit(solution)/shard_map/ppermute | solution.py:15
  57.9 0.7 collective-permute-start.11
  58.6 0.1 copy-done.6
  58.7 6.8 %collective-permute-done.4 = bf16[256,1024]{1,0:T(8,128)(2,1)S(1)} collective-permute-done((bf16[256,1024]{1,0:T(8,128)(2,1)S(1)}, bf16[256,1024]{1,0:T(8,128)(2,1)S(1)}, u32[]{:S(2)}, u32[]{:S(2)}) %collective-permute-start.4) | collective-permute-done | bytes 524320 | tf_op jit(solution)/shard_map/ppermute | solution.py:15
  65.5 6.6 %collective-permute-start.5 = (bf16[256,1024]{1,0:T(8,128)(2,1)S(1)}, bf16[256,1024]{1,0:T(8,128)(2,1)S(1)}, u32[]{:S(2)}, u32[]{:S(2)}) collective-permute-start(bf16[256,1024]{1,0:T(8,128)(2,1)S(1)} %collective-permute-done.4), channel_id=1, source_target_pairs={{0,1},{1,2},{2,3},{3,4},{4,5},{5,6},{6,7},{7,8},{8,9},{9,10},{10,1... | collective-permute-start | bytes 1572872 | tf_op jit(solution)/shard_map/ppermute | solution.py:15
  72.1 0.8 copy-done.8
  72.9 3.9 %collective-permute-done.5 = bf16[256,1024]{1,0:T(8,128)(2,1)S(1)} collective-permute-done((bf16[256,1024]{1,0:T(8,128)(2,1)S(1)}, bf16[256,1024]{1,0:T(8,128)(2,1)S(1)}, u32[]{:S(2)}, u32[]{:S(2)}) %collective-permute-start.5) | collective-permute-done | bytes 524320 | tf_op jit(solution)/shard_map/ppermute | solution.py:15
  76.8 9.6 %collective-permute-start.6 = (bf16[256,1024]{1,0:T(8,128)(2,1)S(1)}, bf16[256,1024]{1,0:T(8,128)(2,1)}, u32[]{:S(2)}, u32[]{:S(2)}) collective-permute-start(bf16[256,1024]{1,0:T(8,128)(2,1)S(1)} %collective-permute-done.5), channel_id=1, source_target_pairs={{0,1},{1,2},{2,3},{3,4},{4,5},{5,6},{6,7},{7,8},{8,9},{9,10},{10,1... | collective-permute-start | bytes 1572872 | tf_op jit(solution)/shard_map/ppermute | solution.py:15
  86.4 4.6 %collective-permute-done.6 = bf16[256,1024]{1,0:T(8,128)(2,1)} collective-permute-done((bf16[256,1024]{1,0:T(8,128)(2,1)S(1)}, bf16[256,1024]{1,0:T(8,128)(2,1)}, u32[]{:S(2)}, u32[]{:S(2)}) %collective-permute-start.6) | collective-permute-done | bytes 524320 | tf_op jit(solution)/shard_map/ppermute | solution.py:15
  91.0 9.6 %collective-permute-start.7 = (bf16[256,1024]{1,0:T(8,128)(2,1)}, bf16[256,1024]{1,0:T(8,128)(2,1)}, u32[]{:S(2)}, u32[]{:S(2)}) collective-permute-start(bf16[256,1024]{1,0:T(8,128)(2,1)} %collective-permute-done.6), channel_id=1, source_target_pairs={{0,1},{1,2},{2,3},{3,4},{4,5},{5,6},{6,7},{7,8},{8,9},{9,10},{10,1... | collective-permute-start | bytes 1572872 | tf_op jit(solution)/shard_map/ppermute | solution.py:15
  100.6 1.7 convolution_convert_fusion
  102.4 2.3 collective-permute-done.7
  104.7 1.1 constant_dynamic-update-slice_fusion.31
  105.7 1.1 constant_dynamic-update-slice_fusion.30
  106.8 1.1 constant_dynamic-update-slice_fusion.29
  107.9 1.1 constant_dynamic-update-slice_fusion.28
  109.0 1.1 constant_dynamic-update-slice_fusion.27
  110.1 1.1 constant_dynamic-update-slice_fusion.26
  111.2 1.1 constant_dynamic-update-slice_fusion.23
  112.4 1.1 constant_dynamic-update-slice_fusion.20
  113.5 1.1 constant_dynamic-update-slice_fusion.19
  114.6 1.1 constant_dynamic-update-slice_fusion.18
  115.7 1.1 constant_dynamic-update-slice_fusion.17
  116.8 1.1 constant_dynamic-update-slice_fusion.15
  117.9 1.1 constant_dynamic-update-slice_fusion.14
  119.6 1.1 constant_dynamic-update-slice_fusion.2
  120.6 1.1 constant_dynamic-update-slice_fusion.1
  121.8 5.7 %copy-done.1 = bf16[8192,1024]{1,0:T(8,128)(2,1)} copy-done((bf16[8192,1024]{1,0:T(8,128)(2,1)}, bf16[8192,1024]{1,0:T(8,128)(2,1)S(1)}, u32[]{:S(2)}) %copy-start.1) | copy-done | bytes 16777240
  127.5 2.7 fusion.7
  130.2 31.5 %all-gather = bf16[65536]{0:T(1024)(128)(2,1)S(1)} all-gather(bf16[4096]{0:T(1024)(128)(2,1)S(1)} %fusion.7), channel_id=2, replica_groups=mesh['parts'=2,'chol'=16] {'chol'}, dimensions={0}, use_global_device_ids=true | all-gather | bytes 139264 | tf_op jit(solution)/shard_map/all_gather | solution.py:52
  161.8 0.3 fusion.60
  162.0 1.6 fusion.47
  163.7 87.2 %all-reduce.2.cloned.1.call-done = f32[16,4096]{1,0:T(8,128)} async-done(((f32[16,4096]{1,0:T(8,128)}), f32[16,4096]{1,0:T(8,128)}) %all-reduce.2.cloned.1.call-update) | async-done | bytes 262160 | tf_op jit(solution)/shard_map/psum | solution.py:58
  250.9 0.9 constant_dynamic-slice_fusion
  251.8 10.7 %fusion.8 = f32[100,1024]{1,0:T(8,128)S(1)} fusion(f32[4096]{0:T(1024)S(1)} %bitcast.25, bf16[8192,1024]{1,0:T(8,128)(2,1)} %copy-done.1, s32[]{:T(128)S(6)} %select_n.17, f32[1,100,1024]{2,0,1:T(1,128)S(1)} %copy-done.2), kind=kOutput, calls=%fused_computation.14 | convolution fusion | flops 1678540800 | bytes 17613824 | tf_op jit(solution)/shard_map/while/body/eval_jaxpr/dot_general | solution.py:40
  262.5 9.9 %fusion.13 = f32[100,1024]{1,0:T(8,128)S(1)} fusion(bf16[8192,1024]{1,0:T(8,128)(2,1)} %copy-done.1, s32[]{:T(128)S(6)} %select_n.17, f32[4096]{0:T(1024)S(1)} %bitcast.26, f32[100,1024]{1,0:T(8,128)S(1)} %fusion.8), kind=kOutput, calls=%fused_computation.19 | convolution fusion | flops 1679052800 | bytes 17613824 | tf_op jit(solution)/shard_map/while/body/eval_jaxpr/dot_general | solution.py:40
  272.4 9.9 %fusion.10 = f32[100,1024]{1,0:T(8,128)S(1)} fusion(bf16[8192,1024]{1,0:T(8,128)(2,1)} %copy-done.1, s32[]{:T(128)S(6)} %select_n.17, f32[4096]{0:T(1024)S(1)} %bitcast.27, f32[100,1024]{1,0:T(8,128)S(1)} %fusion.13), kind=kOutput, calls=%fused_computation.16 | convolution fusion | flops 1679052800 | bytes 17613824 | tf_op jit(solution)/shard_map/while/body/eval_jaxpr/dot_general | solution.py:40
  282.3 10.1 %fusion.31 = f32[1,100,1024]{2,1,0:T(8,128)S(1)} fusion(f32[100,1024]{1,0:T(8,128)S(1)} %fusion.10, f32[100,1024]{1,0:T(8,128)S(1)} %fusion.13, f32[100,1024]{1,0:T(8,128)S(1)} %fusion.8, f32[1,100,1024]{2,0,1:T(1,128)S(1)} %copy-done.2, bf16[8192,1024]{1,0:T(8,128)(2,1)} %copy-done.1, s32[]{:T(128)S(6)} %select_n.17, f32[4096]{0:T(1024)S(1)} %bitcast.28), kind=kOutput, calls=%fused_computation.32 | convolution fusion | flops 1679462400 | bytes 19317760 | tf_op jit(solution)/shard_map/while/body/eval_jaxpr/dot_general | solution.py:40
  292.4 1.2 copy.9
  (65 shorter events, 0.9 us)
Async XLA Ops:
  7.2 154.6 %copy-start = (bf16[64,4096]{1,0:T(8,128)(2,1)S(1)}, bf16[64,4096]{1,0:T(8,128)(2,1)}, u32[]{:S(2)}) copy-start(bf16[64,4096]{1,0:T(8,128)(2,1)} %param.10) | copy-start | bytes 1572868
  7.2 112.1 %copy-start.3 = (bf16[256,1024]{1,0:T(8,128)(2,1)S(1)}, bf16[256,1024]{1,0:T(8,128)(2,1)}, u32[]{:S(2)}) copy-start(bf16[256,1024]{1,0:T(8,128)(2,1)} %param.8) | copy-start | bytes 1572868
  7.2 243.7 %all-reduce.2.cloned.1.call-start = ((), (), s32[]{:S(2)}) async-start(), calls=%async_computation | async-start | bytes 524288 | tf_op jit(solution)/shard_map/psum | solution.py:58
  7.2 12.6 %collective-permute-start = (bf16[256,1024]{1,0:T(8,128)(2,1)}, bf16[256,1024]{1,0:T(8,128)(2,1)S(1)}, u32[]{:S(2)}, u32[]{:S(2)}) collective-permute-start(bf16[256,1024]{1,0:T(8,128)(2,1)} %param.8), channel_id=1, source_target_pairs={{0,1},{1,2},{2,3},{3,4},{4,5},{5,6},{6,7},{7,8},{8,9},{9,10},{10,1... | collective-permute-start | bytes 1572872 | tf_op jit(solution)/shard_map/ppermute | solution.py:15
  19.8 11.4 %collective-permute-start.1 = (bf16[256,1024]{1,0:T(8,128)(2,1)S(1)}, bf16[256,1024]{1,0:T(8,128)(2,1)S(1)}, u32[]{:S(2)}, u32[]{:S(2)}) collective-permute-start(bf16[256,1024]{1,0:T(8,128)(2,1)S(1)} %collective-permute-done), channel_id=1, source_target_pairs={{0,1},{1,2},{2,3},{3,4},{4,5},{5,6},{6,7},{7,8},{8,9},{9,10},{10,1... | collective-permute-start | bytes 1572872 | tf_op jit(solution)/shard_map/ppermute | solution.py:15
  19.8 11.5 %collective-permute-start.8 = (bf16[256,1024]{1,0:T(8,128)(2,1)}, bf16[256,1024]{1,0:T(8,128)(2,1)S(1)}, u32[]{:S(2)}, u32[]{:S(2)}) collective-permute-start(bf16[256,1024]{1,0:T(8,128)(2,1)} %param.8), channel_id=1, source_target_pairs={{0,15},{1,0},{2,1},{3,2},{4,3},{5,4},{6,5},{7,6},{8,7},{9,8},{10,9... | collective-permute-start | bytes 1572872 | tf_op jit(solution)/shard_map/ppermute | solution.py:17
  31.2 11.4 %collective-permute-start.2 = (bf16[256,1024]{1,0:T(8,128)(2,1)S(1)}, bf16[256,1024]{1,0:T(8,128)(2,1)S(1)}, u32[]{:S(2)}, u32[]{:S(2)}) collective-permute-start(bf16[256,1024]{1,0:T(8,128)(2,1)S(1)} %collective-permute-done.1), channel_id=1, source_target_pairs={{0,1},{1,2},{2,3},{3,4},{4,5},{5,6},{6,7},{7,8},{8,9},{9,10},{10,1... | collective-permute-start | bytes 1572872 | tf_op jit(solution)/shard_map/ppermute | solution.py:15
  31.3 13.1 %collective-permute-start.9 = (bf16[256,1024]{1,0:T(8,128)(2,1)S(1)}, bf16[256,1024]{1,0:T(8,128)(2,1)S(1)}, u32[]{:S(2)}, u32[]{:S(2)}) collective-permute-start(bf16[256,1024]{1,0:T(8,128)(2,1)S(1)} %collective-permute-done.8), channel_id=1, source_target_pairs={{0,15},{1,0},{2,1},{3,2},{4,3},{5,4},{6,5},{7,6},{8,7},{9,8},{10,9... | collective-permute-start | bytes 1572872 | tf_op jit(solution)/shard_map/ppermute | solution.py:17
  42.7 15.2 %copy-start.4 = (bf16[256,1024]{1,0:T(8,128)(2,1)}, bf16[256,1024]{1,0:T(8,128)(2,1)S(1)}, u32[]{:S(2)}) copy-start(bf16[256,1024]{1,0:T(8,128)(2,1)S(1)} %collective-permute-done.2) | copy-start | bytes 1572868
  42.7 11.4 %collective-permute-start.3 = (bf16[256,1024]{1,0:T(8,128)(2,1)S(1)}, bf16[256,1024]{1,0:T(8,128)(2,1)S(1)}, u32[]{:S(2)}, u32[]{:S(2)}) collective-permute-start(bf16[256,1024]{1,0:T(8,128)(2,1)S(1)} %collective-permute-done.2), channel_id=1, source_target_pairs={{0,1},{1,2},{2,3},{3,4},{4,5},{5,6},{6,7},{7,8},{8,9},{9,10},{10,1... | collective-permute-start | bytes 1572872 | tf_op jit(solution)/shard_map/ppermute | solution.py:15
  44.4 13.5 %collective-permute-start.10 = (bf16[256,1024]{1,0:T(8,128)(2,1)S(1)}, bf16[256,1024]{1,0:T(8,128)(2,1)S(1)}, u32[]{:S(2)}, u32[]{:S(2)}) collective-permute-start(bf16[256,1024]{1,0:T(8,128)(2,1)S(1)} %collective-permute-done.9), channel_id=1, source_target_pairs={{0,15},{1,0},{2,1},{3,2},{4,3},{5,4},{6,5},{7,6},{8,7},{9,8},{10,9... | collective-permute-start | bytes 1572872 | tf_op jit(solution)/shard_map/ppermute | solution.py:17
  54.1 32.3 %copy-start.10 = (bf16[256,1024]{1,0:T(8,128)(2,1)}, bf16[256,1024]{1,0:T(8,128)(2,1)S(1)}, u32[]{:S(2)}) copy-start(bf16[256,1024]{1,0:T(8,128)(2,1)S(1)} %collective-permute-done.3) | copy-start | bytes 1572868
  54.1 11.4 %collective-permute-start.4 = (bf16[256,1024]{1,0:T(8,128)(2,1)S(1)}, bf16[256,1024]{1,0:T(8,128)(2,1)S(1)}, u32[]{:S(2)}, u32[]{:S(2)}) collective-permute-start(bf16[256,1024]{1,0:T(8,128)(2,1)S(1)} %collective-permute-done.3), channel_id=1, source_target_pairs={{0,1},{1,2},{2,3},{3,4},{4,5},{5,6},{6,7},{7,8},{8,9},{9,10},{10,1... | collective-permute-start | bytes 1572872 | tf_op jit(solution)/shard_map/ppermute | solution.py:15
  57.9 0.8 copy-start.6
  57.9 14.2 %collective-permute-start.11 = (bf16[256,1024]{1,0:T(8,128)(2,1)S(1)}, bf16[256,1024]{1,0:T(8,128)(2,1)S(1)}, u32[]{:S(2)}, u32[]{:S(2)}) collective-permute-start(bf16[256,1024]{1,0:T(8,128)(2,1)S(1)} %collective-permute-done.10), channel_id=1, source_target_pairs={{0,15},{1,0},{2,1},{3,2},{4,3},{5,4},{6,5},{7,6},{8,7},{9,8},{10,9... | collective-permute-start | bytes 1572872 | tf_op jit(solution)/shard_map/ppermute | solution.py:17
  65.5 20.9 %copy-start.12 = (bf16[256,1024]{1,0:T(8,128)(2,1)}, bf16[256,1024]{1,0:T(8,128)(2,1)S(1)}, u32[]{:S(2)}) copy-start(bf16[256,1024]{1,0:T(8,128)(2,1)S(1)} %collective-permute-done.4) | copy-start | bytes 1572868
  65.5 11.3 %collective-permute-start.5 = (bf16[256,1024]{1,0:T(8,128)(2,1)S(1)}, bf16[256,1024]{1,0:T(8,128)(2,1)S(1)}, u32[]{:S(2)}, u32[]{:S(2)}) collective-permute-start(bf16[256,1024]{1,0:T(8,128)(2,1)S(1)} %collective-permute-done.4), channel_id=1, source_target_pairs={{0,1},{1,2},{2,3},{3,4},{4,5},{5,6},{6,7},{7,8},{8,9},{9,10},{10,1... | collective-permute-start | bytes 1572872 | tf_op jit(solution)/shard_map/ppermute | solution.py:15
  72.1 0.8 copy-start.8
  72.9 13.4 %collective-permute-start.12 = (bf16[256,1024]{1,0:T(8,128)(2,1)S(1)}, bf16[256,1024]{1,0:T(8,128)(2,1)}, u32[]{:S(2)}, u32[]{:S(2)}) collective-permute-start(bf16[256,1024]{1,0:T(8,128)(2,1)S(1)} %collective-permute-done.11), channel_id=1, source_target_pairs={{0,15},{1,0},{2,1},{3,2},{4,3},{5,4},{6,5},{7,6},{8,7},{9,8},{10,9... | collective-permute-start | bytes 1572872 | tf_op jit(solution)/shard_map/ppermute | solution.py:17
  76.8 14.2 %copy-start.14 = (bf16[256,1024]{1,0:T(8,128)(2,1)}, bf16[256,1024]{1,0:T(8,128)(2,1)S(1)}, u32[]{:S(2)}) copy-start(bf16[256,1024]{1,0:T(8,128)(2,1)S(1)} %collective-permute-done.5) | copy-start | bytes 1572868
  76.8 14.2 %collective-permute-start.6 = (bf16[256,1024]{1,0:T(8,128)(2,1)S(1)}, bf16[256,1024]{1,0:T(8,128)(2,1)}, u32[]{:S(2)}, u32[]{:S(2)}) collective-permute-start(bf16[256,1024]{1,0:T(8,128)(2,1)S(1)} %collective-permute-done.5), channel_id=1, source_target_pairs={{0,1},{1,2},{2,3},{3,4},{4,5},{5,6},{6,7},{7,8},{8,9},{9,10},{10,1... | collective-permute-start | bytes 1572872 | tf_op jit(solution)/shard_map/ppermute | solution.py:15
  86.3 16.0 %collective-permute-start.13 = (bf16[256,1024]{1,0:T(8,128)(2,1)}, bf16[256,1024]{1,0:T(8,128)(2,1)}, u32[]{:S(2)}, u32[]{:S(2)}) collective-permute-start(bf16[256,1024]{1,0:T(8,128)(2,1)} %collective-permute-done.12), channel_id=1, source_target_pairs={{0,15},{1,0},{2,1},{3,2},{4,3},{5,4},{6,5},{7,6},{8,7},{9,8},{10,9... | collective-permute-start | bytes 1572872 | tf_op jit(solution)/shard_map/ppermute | solution.py:17
  91.0 13.7 %collective-permute-start.7 = (bf16[256,1024]{1,0:T(8,128)(2,1)}, bf16[256,1024]{1,0:T(8,128)(2,1)}, u32[]{:S(2)}, u32[]{:S(2)}) collective-permute-start(bf16[256,1024]{1,0:T(8,128)(2,1)} %collective-permute-done.6), channel_id=1, source_target_pairs={{0,1},{1,2},{2,3},{3,4},{4,5},{5,6},{6,7},{7,8},{8,9},{9,10},{10,1... | collective-permute-start | bytes 1572872 | tf_op jit(solution)/shard_map/ppermute | solution.py:15
  100.6 18.5 %copy-start.15 = (bf16[256,1024]{1,0:T(8,128)(2,1)S(1)}, bf16[256,1024]{1,0:T(8,128)(2,1)}, u32[]{:S(2)}) copy-start(bf16[256,1024]{1,0:T(8,128)(2,1)} %copy-done.14) | copy-start | bytes 1572868
  100.6 18.5 %copy-start.13 = (bf16[256,1024]{1,0:T(8,128)(2,1)S(1)}, bf16[256,1024]{1,0:T(8,128)(2,1)}, u32[]{:S(2)}) copy-start(bf16[256,1024]{1,0:T(8,128)(2,1)} %copy-done.12) | copy-start | bytes 1572868
  100.6 18.6 %copy-start.11 = (bf16[256,1024]{1,0:T(8,128)(2,1)S(1)}, bf16[256,1024]{1,0:T(8,128)(2,1)}, u32[]{:S(2)}) copy-start(bf16[256,1024]{1,0:T(8,128)(2,1)} %copy-done.10) | copy-start | bytes 1572868
  100.6 18.6 %copy-start.5 = (bf16[256,1024]{1,0:T(8,128)(2,1)S(1)}, bf16[256,1024]{1,0:T(8,128)(2,1)}, u32[]{:S(2)}) copy-start(bf16[256,1024]{1,0:T(8,128)(2,1)} %copy-done.4) | copy-start | bytes 1572868
  100.6 18.9 %copy-start.7 = (bf16[256,1024]{1,0:T(8,128)(2,1)S(1)}, bf16[256,1024]{1,0:T(8,128)(2,1)}, u32[]{:S(2)}) copy-start(bf16[256,1024]{1,0:T(8,128)(2,1)} %copy-done.6) | copy-start | bytes 1572868
  100.6 18.9 %copy-start.9 = (bf16[256,1024]{1,0:T(8,128)(2,1)S(1)}, bf16[256,1024]{1,0:T(8,128)(2,1)}, u32[]{:S(2)}) copy-start(bf16[256,1024]{1,0:T(8,128)(2,1)} %copy-done.8) | copy-start | bytes 1572868
  102.3 25.2 %copy-start.17 = (bf16[100,4096]{1,0:T(8,128)(2,1)S(1)}, bf16[100,4096]{1,0:T(8,128)(2,1)}, u32[]{:S(2)}) copy-start(bf16[100,4096]{1,0:T(8,128)(2,1)} %param.9) | copy-start | bytes 2457604
  102.3 14.5 %collective-permute-start.14 = (bf16[256,1024]{1,0:T(8,128)(2,1)}, bf16[256,1024]{1,0:T(8,128)(2,1)S(1)}, u32[]{:S(2)}, u32[]{:S(2)}) collective-permute-start(bf16[256,1024]{1,0:T(8,128)(2,1)} %collective-permute-done.13), channel_id=1, source_target_pairs={{0,15},{1,0},{2,1},{3,2},{4,3},{5,4},{6,5},{7,6},{8,7},{9,8},{10,9... | collective-permute-start | bytes 1572872 | tf_op jit(solution)/shard_map/ppermute | solution.py:17
  115.6 136.1 %copy-start.2 = (f32[1,100,1024]{2,0,1:T(1,128)S(1)}, f32[1,100,1024]{2,0,1:T(1,128)}, u32[]{:S(2)}) copy-start(f32[1,100,1024]{2,0,1:T(1,128)} %param.6) | copy-start | bytes 1228804
  121.8 5.7 %copy-start.1 = (bf16[8192,1024]{1,0:T(8,128)(2,1)}, bf16[8192,1024]{1,0:T(8,128)(2,1)S(1)}, u32[]{:S(2)}) copy-start(bf16[8192,1024]{1,0:T(8,128)(2,1)S(1)} %constant_dynamic-update-slice_fusion) | copy-start | bytes 50331652
  162.0 110.3 %copy-start.16 = (f32[16,64]{1,0:T(8,128)}, f32[16,64]{1,0:T(8,128)S(1)}, u32[]{:S(2)}) copy-start(f32[16,64]{1,0:T(8,128)S(1)} %fusion.60) | copy-start | bytes 12292
Sparse Core Ops, SparseCore 0:
  163.8 87.0 all-reduce.1
